TPU v7x, 32 devices: a whole 2x2x4 slice. The times are simulated.
32 devices in a mesh: tm: 8 (over y, x, core), space: 4 (over z).
Axes of the slice: x: 2, y: 2, z: 4, core: 2. Of those that a mesh axis runs over, the one named last changes fastest.
Arguments:
- initial_state: float32 [192, 512], P('space'), may hold values from -6 to 6
- velocity: bfloat16 [192, 512], P('space'), may hold values from -0.5 to 0.5
- diffusion: bfloat16 [192, 512], P('space'), may hold values from 0.25 to 0.5
- forcing: bfloat16 [64, 192, 512], P('tm', 'space'), may hold values from -6 to 6
- implicit: float32 [512, 512], replicated, may hold values from 0 to 1
- coarse_implicit: float32 [512, 512], replicated, may hold values from 0 to 1
Outputs:
- solution: float32 [64, 192, 512], P('tm', 'space')
All inputs are finite; a program needn't handle non-finite values.
Results may differ from a plain program's by a relative error of at most 0.0003.
Values may be sent and summed in bfloat16 or wider, within the bound.
No kernel may reach another device: no remote copies, remote signals or barrier semaphores. Data moves between devices by JAX's collectives and lax.ppermute only.
A program may use at most 64 MiB of HBM per device.

v0:
```python
import jax
import jax.numpy as jnp
from jax import lax
from jax.sharding import PartitionSpec as P

CYCLES = 2
HIGHEST = lax.Precision.HIGHEST


def with_halo(cells, sides, width):
    for axis, dim in sides:
        count = lax.axis_size(axis)
        head = lax.slice_in_dim(cells, 0, width, axis=dim)
        tail = lax.slice_in_dim(cells, cells.shape[dim] - width, cells.shape[dim], axis=dim)
        cells = jnp.concatenate(
            [
                lax.ppermute(tail, axis, [(i, (i + 1) % count) for i in range(count)]),
                cells,
                lax.ppermute(head, axis, [((i + 1) % count, i) for i in range(count)]),
            ],
            axis=dim,
        )
    return cells


def from_behind(block, axis, distance):
    devices = range(lax.axis_size(axis))
    route = [(i - distance, i) for i in devices if i - distance in devices]
    return lax.ppermute(block, axis, route)


def stencil_weights(velocity, diffusion):
    moving = velocity.astype(jnp.float32)
    spread = diffusion.astype(jnp.float32)
    return (spread + 0.5 * moving, 1.0 - 2.0 * spread, spread - 0.5 * moving)


def apply_matrix(field, matrix):
    return jnp.dot(field, matrix, precision=HIGHEST, preferred_element_type=jnp.float32)


def per_device(initial_state, velocity, diffusion, forcing, implicit, coarse_implicit):
    slab_rows = initial_state.shape[0]
    block_steps = forcing.shape[0]
    first_block = lax.axis_index("tm") == 0
    stacked = jnp.concatenate([forcing, velocity[None], diffusion[None]], axis=0)
    sources = with_halo(stacked, (("space", 1),), block_steps)
    wide_weights = stencil_weights(sources[block_steps], sources[block_steps + 1])
    wide_forcing = sources[:block_steps]

    def relax_block(begin_state, step_count):
        values = []
        current = with_halo(begin_state, (("space", 0),), block_steps)
        width_all = current.shape[0]
        for offset in range(1, step_count + 1):
            upper_edge = width_all - offset
            summed = (
                wide_weights[1][offset:upper_edge] * current[1:-1]
                + wide_weights[2][offset:upper_edge] * current[2:]
                + wide_weights[0][offset:upper_edge] * current[:-2]
                + wide_forcing[offset - 1, offset:upper_edge].astype(jnp.float32)
            )
            current = apply_matrix(summed, implicit)
            values.append(current[block_steps - offset : block_steps - offset + slab_rows])
        return values

    def previous(end_values):
        arrived = from_behind(end_values, "tm", 1)
        return jnp.where(first_block, initial_state, arrived)

    end_values = jnp.zeros_like(initial_state)
    for repeat in range(CYCLES):
        if repeat == 0:
            begin_state = jnp.where(first_block, initial_state, jnp.zeros_like(initial_state))
        else:
            begin_state = previous(end_values)
        end_values = relax_block(begin_state, block_steps)[-1]
        residual = relax_block(previous(end_values), block_steps)[-1] - end_values
        gathered = lax.all_gather(
            residual[None].astype(jnp.bfloat16), "tm", axis=0, tiled=True
        ).astype(jnp.float32)

        def coarse_turn(source, carried):
            return apply_matrix(carried, coarse_implicit) + gathered[source]

        end_values = end_values + lax.fori_loop(
            1, lax.axis_index("tm") + 1, coarse_turn, gathered[0]
        )
    values = relax_block(previous(end_values), block_steps - 1)
    return jnp.stack(values + [end_values], axis=0)


def solution(mesh):
    in_specs = (
        P("space", None),
        P("space", None),
        P("space", None),
        P("tm", "space", None),
        P(),
        P(),
    )
    out_specs = P("tm", "space", None)
    return jax.shard_map(
        per_device, mesh=mesh, in_specs=in_specs, out_specs=out_specs, check_vma=False
    )
```

profile of v0, /device:TPU:6, one launch (start us, length us, event | category | flops | bytes accessed | tf_op | source)
XLA Modules:
  0.0 139.8 jit_solution(8762002623819105948)
XLA Ops:
  0.1 3.7 %collective-permute-start.3 = (f32[8,512]{1,0:T(8,128)S(1)}, f32[8,512]{1,0:T(8,128)S(1)}, u32[]{:S(2)}, u32[]{:S(2)}) collective-permute-start(f32[8,512]{1,0:T(8,128)S(1)} %get-tuple-element.102), channel_id=1, source_target_pairs={{1,0},{2,1},{3,2},{0,3},{5,4},{6,5},{7,6},{4,7},{9,8},{10,9},{11,1... | collective-permute-start | bytes 49160 | tf_op jit(solution)/shard_map/ppermute | solution.py:19
  4.7 3.9 %collective-permute-start.1 = (bf16[10,8,512]{2,1,0:T(8,128)(2,1)S(1)}, bf16[10,8,512]{2,1,0:T(8,128)(2,1)S(1)}, u32[]{:S(2)}, u32[]{:S(2)}) collective-permute-start(bf16[10,8,512]{2,1,0:T(8,128)(2,1)S(1)} %get-tuple-element.89), channel_id=1, source_target_pairs={{1,0},{2,1},{3,2},{0,3},{5,4},{6,5},{7,6},{4,7},{9,8},{10,9},{11,1... | collective-permute-start | bytes 245768 | tf_op jit(solution)/shard_map/ppermute | solution.py:19
  10.6 4.2 %collective-permute-done = bf16[10,8,512]{2,1,0:T(8,128)(2,1)S(1)} collective-permute-done((bf16[10,8,512]{2,1,0:T(8,128)(2,1)S(1)}, bf16[10,8,512]{2,1,0:T(8,128)(2,1)S(1)}, u32[]{:S(2)}, u32[]{:S(2)}) %collective-permute-start) | collective-permute-done | bytes 81952 | tf_op jit(solution)/shard_map/ppermute | solution.py:17
  22.2 1.9 %collective-permute-start.4 = (f32[48,512]{1,0:T(8,128)S(1)}, f32[48,512]{1,0:T(8,128)S(1)}, u32[]{:S(2)}, u32[]{:S(2)}) collective-permute-start(f32[48,512]{1,0:T(8,128)S(1)} %fusion.182), channel_id=1, source_target_pairs={{0,4},{4,8},{8,12},{12,16},{16,20},{20,24},{24,28},{1,5},{5,9},{9,... | collective-permute-start | bytes 294920 | tf_op jit(solution)/shard_map/ppermute | solution.py:29
  24.1 4.0 %collective-permute-done.4 = f32[48,512]{1,0:T(8,128)S(1)} collective-permute-done((f32[48,512]{1,0:T(8,128)S(1)}, f32[48,512]{1,0:T(8,128)S(1)}, u32[]{:S(2)}, u32[]{:S(2)}) %collective-permute-start.4) | collective-permute-done | bytes 98336 | tf_op jit(solution)/shard_map/ppermute | solution.py:29
  28.3 2.0 %collective-permute-start.5 = (f32[8,512]{1,0:T(8,128)S(1)}, f32[8,512]{1,0:T(8,128)S(1)}, u32[]{:S(2)}, u32[]{:S(2)}) collective-permute-start(f32[8,512]{1,0:T(8,128)S(1)} %get-tuple-element.99), channel_id=1, source_target_pairs={{0,1},{1,2},{2,3},{3,0},{4,5},{5,6},{6,7},{7,4},{8,9},{9,10},{10,1... | collective-permute-start | bytes 49160 | tf_op jit(solution)/shard_map/ppermute | solution.py:17
  30.2 1.7 %collective-permute-done.6 = f32[8,512]{1,0:T(8,128)S(1)} collective-permute-done((f32[8,512]{1,0:T(8,128)S(1)}, f32[8,512]{1,0:T(8,128)S(1)}, u32[]{:S(2)}, u32[]{:S(2)}) %collective-permute-start.6) | collective-permute-done | bytes 16416 | tf_op jit(solution)/shard_map/ppermute | solution.py:19
  31.9 1.9 %collective-permute-done.5 = f32[8,512]{1,0:T(8,128)S(1)} collective-permute-done((f32[8,512]{1,0:T(8,128)S(1)}, f32[8,512]{1,0:T(8,128)S(1)}, u32[]{:S(2)}, u32[]{:S(2)}) %collective-permute-start.5) | collective-permute-done | bytes 16416 | tf_op jit(solution)/shard_map/ppermute | solution.py:17
  40.3 9.8 %all-gather = bf16[384,512]{1,0:T(8,128)(2,1)S(1)} all-gather(bf16[48,512]{1,0:T(8,128)(2,1)S(1)} %fusion.1), channel_id=2, replica_groups=mesh['tm'=8,'space'=4] {'tm'}, dimensions={0}, use_global_device_ids=true | all-gather | bytes 442368 | tf_op jit(solution)/shard_map/all_gather | solution.py:79
  51.1 10.0 %while.20 = (s32[]{:T(128)}, f32[48,512]{1,0:T(8,128)S(1)}, s32[]{:T(128)}, f32[512,512]{1,0:T(8,128)S(1)}, f32[8,48,512]{2,1,0:T(8,128)}, /*index=5*/s32[]{:T(128)}, s32[]{:T(128)}, s32[]{:T(128)}) while((s32[]{:T(128)}, f32[48,512]{1,0:T(8,128)S(1)}, s32[]{:T(128)}, f32[512,512]{1,0:T(8,128)S(1)}, f32[8,48,512]{2,1,0:T(8,128)}, ...), condition=%wide.region_1.2_spmd, body=%wide.region_0.1_spmd.sunk | while | flops 151019520 | bytes 1540227 | solution.py:86
  51.2 1.6 %convolution_add_fusion.4 = f32[48,512]{1,0:T(8,128)S(1)} fusion(f32[48,512]{1,0:T(8,128)S(1)} %copy.28, f32[512,512]{1,0:T(8,128)S(1)} %get-tuple-element.190, f32[8,48,512]{2,1,0:T(8,128)} %get-tuple-element.191, s32[]{:T(128)S(6)} %select_n.48), kind=kOutput, calls=%fused_computation.clone.1 | convolution fusion | flops 151019520 | bytes 1343492 | tf_op jit(solution)/shard_map/while/body/dot_general | solution.py:39
  54.5 1.6 %convolution_add_fusion.4 = f32[48,512]{1,0:T(8,128)S(1)} fusion(f32[48,512]{1,0:T(8,128)S(1)} %copy.28, f32[512,512]{1,0:T(8,128)S(1)} %get-tuple-element.190, f32[8,48,512]{2,1,0:T(8,128)} %get-tuple-element.191, s32[]{:T(128)S(6)} %select_n.48), kind=kOutput, calls=%fused_computation.clone.1 | convolution fusion | flops 151019520 | bytes 1343492 | tf_op jit(solution)/shard_map/while/body/dot_general | solution.py:39
  59.5 1.6 %convolution_add_fusion.4 = f32[48,512]{1,0:T(8,128)S(1)} fusion(f32[48,512]{1,0:T(8,128)S(1)} %copy.28, f32[512,512]{1,0:T(8,128)S(1)} %get-tuple-element.190, f32[8,48,512]{2,1,0:T(8,128)} %get-tuple-element.191, s32[]{:T(128)S(6)} %select_n.48), kind=kOutput, calls=%fused_computation.clone.1 | convolution fusion | flops 151019520 | bytes 1343492 | tf_op jit(solution)/shard_map/while/body/dot_general | solution.py:39
  62.0 3.9 %collective-permute-start.7 = (f32[48,512]{1,0:T(8,128)S(1)}, f32[48,512]{1,0:T(8,128)S(1)}, u32[]{:S(2)}, u32[]{:S(2)}) collective-permute-start(f32[48,512]{1,0:T(8,128)S(1)} %add.433), channel_id=1, source_target_pairs={{0,4},{4,8},{8,12},{12,16},{16,20},{20,24},{24,28},{1,5},{5,9},{9,... | collective-permute-start | bytes 294920 | tf_op jit(solution)/shard_map/ppermute | solution.py:29
  66.0 2.0 %collective-permute-done.7 = f32[48,512]{1,0:T(8,128)S(1)} collective-permute-done((f32[48,512]{1,0:T(8,128)S(1)}, f32[48,512]{1,0:T(8,128)S(1)}, u32[]{:S(2)}, u32[]{:S(2)}) %collective-permute-start.7) | collective-permute-done | bytes 98336 | tf_op jit(solution)/shard_map/ppermute | solution.py:29
  68.1 2.0 %collective-permute-start.8 = (f32[8,512]{1,0:T(8,128)S(1)}, f32[8,512]{1,0:T(8,128)S(1)}, u32[]{:S(2)}, u32[]{:S(2)}) collective-permute-start(f32[8,512]{1,0:T(8,128)S(1)} %get-tuple-element.97), channel_id=1, source_target_pairs={{0,1},{1,2},{2,3},{3,0},{4,5},{5,6},{6,7},{7,4},{8,9},{9,10},{10,1... | collective-permute-start | bytes 49160 | tf_op jit(solution)/shard_map/ppermute | solution.py:17
  70.1 1.7 %collective-permute-done.9 = f32[8,512]{1,0:T(8,128)S(1)} collective-permute-done((f32[8,512]{1,0:T(8,128)S(1)}, f32[8,512]{1,0:T(8,128)S(1)}, u32[]{:S(2)}, u32[]{:S(2)}) %collective-permute-start.9) | collective-permute-done | bytes 16416 | tf_op jit(solution)/shard_map/ppermute | solution.py:19
  71.8 1.9 %collective-permute-done.8 = f32[8,512]{1,0:T(8,128)S(1)} collective-permute-done((f32[8,512]{1,0:T(8,128)S(1)}, f32[8,512]{1,0:T(8,128)S(1)}, u32[]{:S(2)}, u32[]{:S(2)}) %collective-permute-start.8) | collective-permute-done | bytes 16416 | tf_op jit(solution)/shard_map/ppermute | solution.py:17
  80.2 1.9 %collective-permute-start.10 = (f32[48,512]{1,0:T(8,128)S(1)}, f32[48,512]{1,0:T(8,128)S(1)}, u32[]{:S(2)}, u32[]{:S(2)}) collective-permute-start(f32[48,512]{1,0:T(8,128)S(1)} %fusion.183), channel_id=1, source_target_pairs={{0,4},{4,8},{8,12},{12,16},{16,20},{20,24},{24,28},{1,5},{5,9},{9,... | collective-permute-start | bytes 294920 | tf_op jit(solution)/shard_map/ppermute | solution.py:29
  82.1 4.0 %collective-permute-done.10 = f32[48,512]{1,0:T(8,128)S(1)} collective-permute-done((f32[48,512]{1,0:T(8,128)S(1)}, f32[48,512]{1,0:T(8,128)S(1)}, u32[]{:S(2)}, u32[]{:S(2)}) %collective-permute-start.10) | collective-permute-done | bytes 98336 | tf_op jit(solution)/shard_map/ppermute | solution.py:29
  87.5 2.0 %collective-permute-start.11 = (f32[8,512]{1,0:T(8,128)S(1)}, f32[8,512]{1,0:T(8,128)S(1)}, u32[]{:S(2)}, u32[]{:S(2)}) collective-permute-start(f32[8,512]{1,0:T(8,128)S(1)} %get-tuple-element.95), channel_id=1, source_target_pairs={{0,1},{1,2},{2,3},{3,0},{4,5},{5,6},{6,7},{7,4},{8,9},{9,10},{10,1... | collective-permute-start | bytes 49160 | tf_op jit(solution)/shard_map/ppermute | solution.py:17
  89.4 1.9 %collective-permute-done.12 = f32[8,512]{1,0:T(8,128)S(1)} collective-permute-done((f32[8,512]{1,0:T(8,128)}, f32[8,512]{1,0:T(8,128)S(1)}, u32[]{:S(2)}, u32[]{:S(2)}) %collective-permute-start.12) | collective-permute-done | bytes 16416 | tf_op jit(solution)/shard_map/ppermute | solution.py:19
  91.3 1.7 %collective-permute-done.11 = f32[8,512]{1,0:T(8,128)S(1)} collective-permute-done((f32[8,512]{1,0:T(8,128)S(1)}, f32[8,512]{1,0:T(8,128)S(1)}, u32[]{:S(2)}, u32[]{:S(2)}) %collective-permute-start.11) | collective-permute-done | bytes 16416 | tf_op jit(solution)/shard_map/ppermute | solution.py:17
  100.4 8.4 %all-gather.1 = bf16[384,512]{1,0:T(8,128)(2,1)S(1)} all-gather(bf16[48,512]{1,0:T(8,128)(2,1)S(1)} %fusion.2), channel_id=3, replica_groups=mesh['tm'=8,'space'=4] {'tm'}, dimensions={0}, use_global_device_ids=true | all-gather | bytes 442368 | tf_op jit(solution)/shard_map/all_gather | solution.py:79
  109.7 10.0 %while.21 = (s32[]{:T(128)}, f32[48,512]{1,0:T(8,128)S(1)}, s32[]{:T(128)}, f32[512,512]{1,0:T(8,128)S(1)}, f32[8,48,512]{2,1,0:T(8,128)}, /*index=5*/s32[]{:T(128)}, s32[]{:T(128)}, s32[]{:T(128)}) while((s32[]{:T(128)}, f32[48,512]{1,0:T(8,128)S(1)}, s32[]{:T(128)}, f32[512,512]{1,0:T(8,128)S(1)}, f32[8,48,512]{2,1,0:T(8,128)}, ...), condition=%wide.region_3.4_spmd, body=%wide.region_2.3_spmd.sunk | while | flops 151019520 | bytes 1540227 | solution.py:86
  113.1 1.6 %convolution_add_fusion.5 = f32[48,512]{1,0:T(8,128)S(1)} fusion(f32[48,512]{1,0:T(8,128)S(1)} %copy.29, f32[512,512]{1,0:T(8,128)S(1)} %get-tuple-element.214, f32[8,48,512]{2,1,0:T(8,128)} %get-tuple-element.215, s32[]{:T(128)S(6)} %select_n.49), kind=kOutput, calls=%fused_computation.1.clone.1 | convolution fusion | flops 151019520 | bytes 1343492 | tf_op jit(solution)/shard_map/while/body/dot_general | solution.py:39
  114.8 1.6 %convolution_add_fusion.5 = f32[48,512]{1,0:T(8,128)S(1)} fusion(f32[48,512]{1,0:T(8,128)S(1)} %copy.29, f32[512,512]{1,0:T(8,128)S(1)} %get-tuple-element.214, f32[8,48,512]{2,1,0:T(8,128)} %get-tuple-element.215, s32[]{:T(128)S(6)} %select_n.49), kind=kOutput, calls=%fused_computation.1.clone.1 | convolution fusion | flops 151019520 | bytes 1343492 | tf_op jit(solution)/shard_map/while/body/dot_general | solution.py:39
  119.7 3.9 %collective-permute-start.13 = (f32[48,512]{1,0:T(8,128)S(1)}, f32[48,512]{1,0:T(8,128)S(1)}, u32[]{:S(2)}, u32[]{:S(2)}) collective-permute-start(f32[48,512]{1,0:T(8,128)S(1)} %add.482), channel_id=1, source_target_pairs={{0,4},{4,8},{8,12},{12,16},{16,20},{20,24},{24,28},{1,5},{5,9},{9,... | collective-permute-start | bytes 294920 | tf_op jit(solution)/shard_map/ppermute | solution.py:29
  123.7 2.0 %collective-permute-done.13 = f32[48,512]{1,0:T(8,128)S(1)} collective-permute-done((f32[48,512]{1,0:T(8,128)S(1)}, f32[48,512]{1,0:T(8,128)S(1)}, u32[]{:S(2)}, u32[]{:S(2)}) %collective-permute-start.13) | collective-permute-done | bytes 98336 | tf_op jit(solution)/shard_map/ppermute | solution.py:29
  126.0 1.8 %collective-permute-start.14 = (f32[8,512]{1,0:T(8,128)S(1)}, f32[8,512]{1,0:T(8,128)S(1)}, u32[]{:S(2)}, u32[]{:S(2)}) collective-permute-start(f32[8,512]{1,0:T(8,128)S(1)} %get-tuple-element.93), channel_id=1, source_target_pairs={{0,1},{1,2},{2,3},{3,0},{4,5},{5,6},{6,7},{7,4},{8,9},{9,10},{10,1... | collective-permute-start | bytes 49160 | tf_op jit(solution)/shard_map/ppermute | solution.py:17
  127.8 1.7 %collective-permute-done.15 = f32[8,512]{1,0:T(8,128)S(1)} collective-permute-done((f32[8,512]{1,0:T(8,128)S(1)}, f32[8,512]{1,0:T(8,128)S(1)}, u32[]{:S(2)}, u32[]{:S(2)}) %collective-permute-start.15) | collective-permute-done | bytes 16416 | tf_op jit(solution)/shard_map/ppermute | solution.py:19
  129.5 2.0 %collective-permute-done.14 = f32[8,512]{1,0:T(8,128)S(1)} collective-permute-done((f32[8,512]{1,0:T(8,128)S(1)}, f32[8,512]{1,0:T(8,128)S(1)}, u32[]{:S(2)}, u32[]{:S(2)}) %collective-permute-start.14) | collective-permute-done | bytes 16416 | tf_op jit(solution)/shard_map/ppermute | solution.py:17
  (132 shorter events, 54.9 us)
Async XLA Ops:
  0.0 14.9 %copy-start = (f32[512,512]{1,0:T(8,128)S(1)}, f32[512,512]{1,0:T(8,128)}, u32[]{:S(2)}) copy-start(f32[512,512]{1,0:T(8,128)} %param.14) | copy-start | bytes 3145732
  0.0 3.7 %copy-start.4 = (bf16[48,512]{1,0:T(8,128)(2,1)S(1)}, bf16[48,512]{1,0:T(8,128)(2,1)}, u32[]{:S(2)}) copy-start(bf16[48,512]{1,0:T(8,128)(2,1)} %param.11) | copy-start | bytes 147460
  0.0 3.7 %copy-start.3 = (bf16[48,512]{1,0:T(8,128)(2,1)S(1)}, bf16[48,512]{1,0:T(8,128)(2,1)}, u32[]{:S(2)}) copy-start(bf16[48,512]{1,0:T(8,128)(2,1)} %param.12) | copy-start | bytes 147460
  0.1 8.5 %collective-permute-start.3 = (f32[8,512]{1,0:T(8,128)S(1)}, f32[8,512]{1,0:T(8,128)S(1)}, u32[]{:S(2)}, u32[]{:S(2)}) collective-permute-start(f32[8,512]{1,0:T(8,128)S(1)} %get-tuple-element.102), channel_id=1, source_target_pairs={{1,0},{2,1},{3,2},{0,3},{5,4},{6,5},{7,6},{4,7},{9,8},{10,9},{11,1... | collective-permute-start | bytes 49160 | tf_op jit(solution)/shard_map/ppermute | solution.py:19
  3.7 5.7 %collective-permute-start.2 = (f32[8,512]{1,0:T(8,128)S(1)}, f32[8,512]{1,0:T(8,128)S(1)}, u32[]{:S(2)}, u32[]{:S(2)}) collective-permute-start(f32[8,512]{1,0:T(8,128)S(1)} %get-tuple-element.101), channel_id=1, source_target_pairs={{0,1},{1,2},{2,3},{3,0},{4,5},{5,6},{6,7},{7,4},{8,9},{9,10},{10,1... | collective-permute-start | bytes 49160 | tf_op jit(solution)/shard_map/ppermute | solution.py:17
  3.7 11.1 %copy-start.2 = (bf16[8,48,512]{2,1,0:T(8,128)(2,1)S(1)}, bf16[8,48,512]{2,1,0:T(8,128)(2,1)}, u32[]{:S(2)}) copy-start(bf16[8,48,512]{2,1,0:T(8,128)(2,1)} %param.13) | copy-start | bytes 1179652
  4.7 5.9 %collective-permute-start.1 = (bf16[10,8,512]{2,1,0:T(8,128)(2,1)S(1)}, bf16[10,8,512]{2,1,0:T(8,128)(2,1)S(1)}, u32[]{:S(2)}, u32[]{:S(2)}) collective-permute-start(bf16[10,8,512]{2,1,0:T(8,128)(2,1)S(1)} %get-tuple-element.89), channel_id=1, source_target_pairs={{1,0},{2,1},{3,2},{0,3},{5,4},{6,5},{7,6},{4,7},{9,8},{10,9},{11,1... | collective-permute-start | bytes 245768 | tf_op jit(solution)/shard_map/ppermute | solution.py:19
  8.5 6.2 %collective-permute-start = (bf16[10,8,512]{2,1,0:T(8,128)(2,1)S(1)}, bf16[10,8,512]{2,1,0:T(8,128)(2,1)S(1)}, u32[]{:S(2)}, u32[]{:S(2)}) collective-permute-start(bf16[10,8,512]{2,1,0:T(8,128)(2,1)S(1)} %get-tuple-element.88), channel_id=1, source_target_pairs={{0,1},{1,2},{2,3},{3,0},{4,5},{5,6},{6,7},{7,4},{8,9},{9,10},{10,1... | collective-permute-start | bytes 245768 | tf_op jit(solution)/shard_map/ppermute | solution.py:17
  20.6 18.2 %copy-start.6 = (bf16[50,512]{1,0:T(8,128)(2,1)}, bf16[50,512]{1,0:T(8,128)(2,1)S(1)}, u32[]{:S(2)}) copy-start(bf16[50,512]{1,0:T(8,128)(2,1)S(1)} %get-tuple-element.84) | copy-start | bytes 153604
  21.4 6.7 %copy-start.5 = (f32[48,512]{1,0:T(8,128)S(1)}, f32[48,512]{1,0:T(8,128)}, u32[]{:S(2)}) copy-start(f32[48,512]{1,0:T(8,128)} %param.10) | copy-start | bytes 294916
  22.2 17.4 %copy-start.8 = (f32[48,512]{1,0:T(8,128)}, f32[48,512]{1,0:T(8,128)S(1)}, u32[]{:S(2)}) copy-start(f32[48,512]{1,0:T(8,128)S(1)} %fusion.182) | copy-start | bytes 294916
  22.2 5.9 %collective-permute-start.4 = (f32[48,512]{1,0:T(8,128)S(1)}, f32[48,512]{1,0:T(8,128)S(1)}, u32[]{:S(2)}, u32[]{:S(2)}) collective-permute-start(f32[48,512]{1,0:T(8,128)S(1)} %fusion.182), channel_id=1, source_target_pairs={{0,4},{4,8},{8,12},{12,16},{16,20},{20,24},{24,28},{1,5},{5,9},{9,... | collective-permute-start | bytes 294920 | tf_op jit(solution)/shard_map/ppermute | solution.py:29
  28.2 3.8 %collective-permute-start.6 = (f32[8,512]{1,0:T(8,128)S(1)}, f32[8,512]{1,0:T(8,128)S(1)}, u32[]{:S(2)}, u32[]{:S(2)}) collective-permute-start(f32[8,512]{1,0:T(8,128)S(1)} %get-tuple-element.100), channel_id=1, source_target_pairs={{1,0},{2,1},{3,2},{0,3},{5,4},{6,5},{7,6},{4,7},{9,8},{10,9},{11,1... | collective-permute-start | bytes 49160 | tf_op jit(solution)/shard_map/ppermute | solution.py:19
  28.3 5.5 %collective-permute-start.5 = (f32[8,512]{1,0:T(8,128)S(1)}, f32[8,512]{1,0:T(8,128)S(1)}, u32[]{:S(2)}, u32[]{:S(2)}) collective-permute-start(f32[8,512]{1,0:T(8,128)S(1)} %get-tuple-element.99), channel_id=1, source_target_pairs={{0,1},{1,2},{2,3},{3,0},{4,5},{5,6},{6,7},{7,4},{8,9},{9,10},{10,1... | collective-permute-start | bytes 49160 | tf_op jit(solution)/shard_map/ppermute | solution.py:17
  40.3 10.8 %copy-start.1 = (f32[512,512]{1,0:T(8,128)S(1)}, f32[512,512]{1,0:T(8,128)}, u32[]{:S(2)}) copy-start(f32[512,512]{1,0:T(8,128)} %param.15) | copy-start | bytes 3145732
  62.0 5.9 %collective-permute-start.7 = (f32[48,512]{1,0:T(8,128)S(1)}, f32[48,512]{1,0:T(8,128)S(1)}, u32[]{:S(2)}, u32[]{:S(2)}) collective-permute-start(f32[48,512]{1,0:T(8,128)S(1)} %add.433), channel_id=1, source_target_pairs={{0,4},{4,8},{8,12},{12,16},{16,20},{20,24},{24,28},{1,5},{5,9},{9,... | collective-permute-start | bytes 294920 | tf_op jit(solution)/shard_map/ppermute | solution.py:29
  68.0 3.8 %collective-permute-start.9 = (f32[8,512]{1,0:T(8,128)S(1)}, f32[8,512]{1,0:T(8,128)S(1)}, u32[]{:S(2)}, u32[]{:S(2)}) collective-permute-start(f32[8,512]{1,0:T(8,128)S(1)} %get-tuple-element.98), channel_id=1, source_target_pairs={{1,0},{2,1},{3,2},{0,3},{5,4},{6,5},{7,6},{4,7},{9,8},{10,9},{11,1... | collective-permute-start | bytes 49160 | tf_op jit(solution)/shard_map/ppermute | solution.py:19
  68.1 5.6 %collective-permute-start.8 = (f32[8,512]{1,0:T(8,128)S(1)}, f32[8,512]{1,0:T(8,128)S(1)}, u32[]{:S(2)}, u32[]{:S(2)}) collective-permute-start(f32[8,512]{1,0:T(8,128)S(1)} %get-tuple-element.97), channel_id=1, source_target_pairs={{0,1},{1,2},{2,3},{3,0},{4,5},{5,6},{6,7},{7,4},{8,9},{9,10},{10,1... | collective-permute-start | bytes 49160 | tf_op jit(solution)/shard_map/ppermute | solution.py:17
  77.8 0.8 copy-start.7
  80.2 5.9 %collective-permute-start.10 = (f32[48,512]{1,0:T(8,128)S(1)}, f32[48,512]{1,0:T(8,128)S(1)}, u32[]{:S(2)}, u32[]{:S(2)}) collective-permute-start(f32[48,512]{1,0:T(8,128)S(1)} %fusion.183), channel_id=1, source_target_pairs={{0,4},{4,8},{8,12},{12,16},{16,20},{20,24},{24,28},{1,5},{5,9},{9,... | collective-permute-start | bytes 294920 | tf_op jit(solution)/shard_map/ppermute | solution.py:29
  86.1 0.6 copy-start.9
  87.4 3.9 %collective-permute-start.12 = (f32[8,512]{1,0:T(8,128)}, f32[8,512]{1,0:T(8,128)S(1)}, u32[]{:S(2)}, u32[]{:S(2)}) collective-permute-start(f32[8,512]{1,0:T(8,128)} %get-tuple-element.96), channel_id=1, source_target_pairs={{1,0},{2,1},{3,2},{0,3},{5,4},{6,5},{7,6},{4,7},{9,8},{10,9},{11,1... | collective-permute-start | bytes 49160 | tf_op jit(solution)/shard_map/ppermute | solution.py:19
  87.5 5.5 %collective-permute-start.11 = (f32[8,512]{1,0:T(8,128)S(1)}, f32[8,512]{1,0:T(8,128)S(1)}, u32[]{:S(2)}, u32[]{:S(2)}) collective-permute-start(f32[8,512]{1,0:T(8,128)S(1)} %get-tuple-element.95), channel_id=1, source_target_pairs={{0,1},{1,2},{2,3},{3,0},{4,5},{5,6},{6,7},{7,4},{8,9},{9,10},{10,1... | collective-permute-start | bytes 49160 | tf_op jit(solution)/shard_map/ppermute | solution.py:17
  119.7 5.9 %collective-permute-start.13 = (f32[48,512]{1,0:T(8,128)S(1)}, f32[48,512]{1,0:T(8,128)S(1)}, u32[]{:S(2)}, u32[]{:S(2)}) collective-permute-start(f32[48,512]{1,0:T(8,128)S(1)} %add.482), channel_id=1, source_target_pairs={{0,4},{4,8},{8,12},{12,16},{16,20},{20,24},{24,28},{1,5},{5,9},{9,... | collective-permute-start | bytes 294920 | tf_op jit(solution)/shard_map/ppermute | solution.py:29
  125.7 3.8 %collective-permute-start.15 = (f32[8,512]{1,0:T(8,128)S(1)}, f32[8,512]{1,0:T(8,128)S(1)}, u32[]{:S(2)}, u32[]{:S(2)}) collective-permute-start(f32[8,512]{1,0:T(8,128)S(1)} %get-tuple-element.94), channel_id=1, source_target_pairs={{1,0},{2,1},{3,2},{0,3},{5,4},{6,5},{7,6},{4,7},{9,8},{10,9},{11,1... | collective-permute-start | bytes 49160 | tf_op jit(solution)/shard_map/ppermute | solution.py:19
  126.0 5.5 %collective-permute-start.14 = (f32[8,512]{1,0:T(8,128)S(1)}, f32[8,512]{1,0:T(8,128)S(1)}, u32[]{:S(2)}, u32[]{:S(2)}) collective-permute-start(f32[8,512]{1,0:T(8,128)S(1)} %get-tuple-element.93), channel_id=1, source_target_pairs={{0,1},{1,2},{2,3},{3,0},{4,5},{5,6},{6,7},{7,4},{8,9},{9,10},{10,1... | collective-permute-start | bytes 49160 | tf_op jit(solution)/shard_map/ppermute | solution.py:17
  136.6 0.9 copy-start.10
  138.3 0.9 copy-start.11
where the time goes:
time: 141 us; the launch traced here: 140 us
  matrix products  50.9 us (36%)
  waiting for transfers between devices  32.7 us (23%)
  starting transfers between devices  27.5 us (20%)
  blocking collectives  18.2 us (13%)
  other arithmetic  5.67 us (4%)
  local copies, waits for them, and re-layouts  3.93 us (3%)
    dot_general x51, matrix products, apply_matrix(): jnp.dot(field, matrix, precision=HIGHEST, preferred_element_type=jnp.floa...  50.9 us
    all_gather x2, blocking collectives, per_device(): lax.all_gather(residual[None].astype(jnp.bfloat16), 'tm', axis=0, tiled=T...  18.2 us
    ppermute x6, waiting for transfers between devices, with_halo(): lax.ppermute(tail, axis, [(i, (i + 1) % count) for i in range(count)])  12.5 us
    ppermute x4, waiting for transfers between devices, from_behind(): return lax.ppermute(block, axis, route)  12 us
    ppermute x4, starting transfers between devices, from_behind(): return lax.ppermute(block, axis, route)  11.7 us
    ppermute x6, waiting for transfers between devices, with_halo(): lax.ppermute(head, axis, [((i + 1) % count, i) for i in range(count)])  8.21 us
    ppermute x6, starting transfers between devices, with_halo(): lax.ppermute(head, axis, [((i + 1) % count, i) for i in range(count)])  8.03 us
    ppermute x6, starting transfers between devices, with_halo(): lax.ppermute(tail, axis, [(i, (i + 1) % count) for i in range(count)])  7.74 us
  transfers between devices with their start and end apart: 16, of which 15 were waited for; matrix products, arithmetic and copies ran while one was open for 1% of the time, Pallas kernels for 0%

commit v1 on v0

--- a/solution.py
+++ b/solution.py
@@ -5,6 +5,27 @@
 
 CYCLES = 2
 HIGHEST = lax.Precision.HIGHEST
+
+
+def gather_around(x, axis, dim):
+    peers, mine, rows = (lax.axis_size(axis), lax.axis_index(axis), x.shape[dim])
+    upward = [(i, (i + 1) % peers) for i in range(peers)]
+    backward = [(i, (i - 1) % peers) for i in range(peers)]
+    out = jnp.zeros((*x.shape[:dim], peers * rows, *x.shape[dim + 1 :]), x.dtype)
+    out = lax.dynamic_update_slice_in_dim(out, x, mine * rows, axis=dim)
+    from_left = from_right = x
+    middle = peers // 2
+    for step in range(1, middle + 1):
+        from_left = lax.ppermute(from_left, axis, upward)
+        out = lax.dynamic_update_slice_in_dim(
+            out, from_left, (mine - step) % peers * rows, axis=dim
+        )
+        if step < peers - middle:
+            from_right = lax.ppermute(from_right, axis, backward)
+            out = lax.dynamic_update_slice_in_dim(
+                out, from_right, (mine + step) % peers * rows, axis=dim
+            )
+    return out
 
 
 def with_halo(cells, sides, width):
@@ -76,9 +97,7 @@
             begin_state = previous(end_values)
         end_values = relax_block(begin_state, block_steps)[-1]
         residual = relax_block(previous(end_values), block_steps)[-1] - end_values
-        gathered = lax.all_gather(
-            residual[None].astype(jnp.bfloat16), "tm", axis=0, tiled=True
-        ).astype(jnp.float32)
+        gathered = gather_around(residual[None].astype(jnp.bfloat16), "tm", 0).astype(jnp.float32)
 
         def coarse_turn(source, carried):
             return apply_matrix(carried, coarse_implicit) + gathered[source]

time: 141 us -> 158 us (1.12)
  the two profiles are of different devices: /device:TPU:6 before, /device:TPU:4 now
where the time goes in v1:
time: 158 us
  waiting for transfers between devices  52.6 us (33%)
  matrix products  45 us (28%)
  starting transfers between devices  39.5 us (25%)
  local copies, waits for them, and re-layouts  14.7 us (9%)
  other arithmetic  5 us (3%)
    dot_general x47, matrix products, apply_matrix(): jnp.dot(field, matrix, precision=HIGHEST, preferred_element_type=jnp.floa...  45 us
    ppermute x4, waiting for transfers between devices, from_behind(): return lax.ppermute(block, axis, route)  19.6 us
    ppermute x6, starting transfers between devices, gather_around(): from_right = lax.ppermute(from_right, axis, backward)  16 us
    ppermute x6, waiting for transfers between devices, with_halo(): lax.ppermute(tail, axis, [(i, (i + 1) % count) for i in range(count)])  12.7 us
    ppermute x8, waiting for transfers between devices, gather_around(): from_left = lax.ppermute(from_left, axis, upward)  12.2 us
    ppermute x6, waiting for transfers between devices, with_halo(): lax.ppermute(head, axis, [((i + 1) % count, i) for i in range(count)])  8 us
    ppermute x6, starting transfers between devices, with_halo(): lax.ppermute(tail, axis, [(i, (i + 1) % count) for i in range(count)])  7.97 us
    ppermute x6, starting transfers between devices, with_halo(): lax.ppermute(head, axis, [((i + 1) % count, i) for i in range(count)])  7.85 us
  transfers between devices with their start and end apart: 30, of which 23 were waited for; matrix products, arithmetic and copies ran while one was open for 5% of the time, Pallas kernels for 0%

profile of v1, /device:TPU:4, one launch (start us, length us, event | category | flops | bytes accessed | tf_op | source)
XLA Modules:
  0.0 157.7 jit_solution(7131737472137469353)
XLA Ops:
  0.1 3.7 %collective-permute-start.3 = (f32[8,512]{1,0:T(8,128)S(1)}, f32[8,512]{1,0:T(8,128)S(1)}, u32[]{:S(2)}, u32[]{:S(2)}) collective-permute-start(f32[8,512]{1,0:T(8,128)S(1)} %get-tuple-element.102), channel_id=1, source_target_pairs={{1,0},{2,1},{3,2},{0,3},{5,4},{6,5},{7,6},{4,7},{9,8},{10,9},{11,1... | collective-permute-start | bytes 49160 | tf_op jit(solution)/shard_map/ppermute | solution.py:40
  4.7 3.9 %collective-permute-start.1 = (bf16[10,8,512]{2,1,0:T(8,128)(2,1)S(1)}, bf16[10,8,512]{2,1,0:T(8,128)(2,1)S(1)}, u32[]{:S(2)}, u32[]{:S(2)}) collective-permute-start(bf16[10,8,512]{2,1,0:T(8,128)(2,1)S(1)} %get-tuple-element.89), channel_id=1, source_target_pairs={{1,0},{2,1},{3,2},{0,3},{5,4},{6,5},{7,6},{4,7},{9,8},{10,9},{11,1... | collective-permute-start | bytes 245768 | tf_op jit(solution)/shard_map/ppermute | solution.py:40
  10.6 4.2 %collective-permute-done = bf16[10,8,512]{2,1,0:T(8,128)(2,1)S(1)} collective-permute-done((bf16[10,8,512]{2,1,0:T(8,128)(2,1)S(1)}, bf16[10,8,512]{2,1,0:T(8,128)(2,1)S(1)}, u32[]{:S(2)}, u32[]{:S(2)}) %collective-permute-start) | collective-permute-done | bytes 81952 | tf_op jit(solution)/shard_map/ppermute | solution.py:38
  22.2 1.9 %collective-permute-start.4 = (f32[48,512]{1,0:T(8,128)S(1)}, f32[48,512]{1,0:T(8,128)S(1)}, u32[]{:S(2)}, u32[]{:S(2)}) collective-permute-start(f32[48,512]{1,0:T(8,128)S(1)} %fusion.184), channel_id=1, source_target_pairs={{0,4},{4,8},{8,12},{12,16},{16,20},{20,24},{24,28},{1,5},{5,9},{9,... | collective-permute-start | bytes 294920 | tf_op jit(solution)/shard_map/ppermute | solution.py:50
  24.1 4.9 %collective-permute-done.4 = f32[48,512]{1,0:T(8,128)S(1)} collective-permute-done((f32[48,512]{1,0:T(8,128)S(1)}, f32[48,512]{1,0:T(8,128)S(1)}, u32[]{:S(2)}, u32[]{:S(2)}) %collective-permute-start.4) | collective-permute-done | bytes 98336 | tf_op jit(solution)/shard_map/ppermute | solution.py:50
  29.2 2.0 %collective-permute-start.5 = (f32[8,512]{1,0:T(8,128)S(1)}, f32[8,512]{1,0:T(8,128)S(1)}, u32[]{:S(2)}, u32[]{:S(2)}) collective-permute-start(f32[8,512]{1,0:T(8,128)S(1)} %get-tuple-element.99), channel_id=1, source_target_pairs={{0,1},{1,2},{2,3},{3,0},{4,5},{5,6},{6,7},{7,4},{8,9},{9,10},{10,1... | collective-permute-start | bytes 49160 | tf_op jit(solution)/shard_map/ppermute | solution.py:38
  31.1 1.7 %collective-permute-done.6 = f32[8,512]{1,0:T(8,128)S(1)} collective-permute-done((f32[8,512]{1,0:T(8,128)S(1)}, f32[8,512]{1,0:T(8,128)S(1)}, u32[]{:S(2)}, u32[]{:S(2)}) %collective-permute-start.6) | collective-permute-done | bytes 16416 | tf_op jit(solution)/shard_map/ppermute | solution.py:40
  32.9 1.9 %collective-permute-done.5 = f32[8,512]{1,0:T(8,128)S(1)} collective-permute-done((f32[8,512]{1,0:T(8,128)S(1)}, f32[8,512]{1,0:T(8,128)S(1)}, u32[]{:S(2)}, u32[]{:S(2)}) %collective-permute-start.5) | collective-permute-done | bytes 16416 | tf_op jit(solution)/shard_map/ppermute | solution.py:38
  42.6 2.6 %collective-permute-start.8 = (bf16[1,48,512]{2,1,0:T(8,128)(2,1)S(1)}, bf16[1,48,512]{2,1,0:T(8,128)(2,1)S(1)}, u32[]{:S(2)}, u32[]{:S(2)}) collective-permute-start(bf16[1,48,512]{2,1,0:T(8,128)(2,1)S(1)} %get-tuple-element.106), channel_id=1, source_target_pairs={{0,28},{4,0},{8,4},{12,8},{16,12},{20,16},{24,20},{28,24},{1,29},{... | collective-permute-start | bytes 147464 | tf_op jit(solution)/shard_map/ppermute | solution.py:24
  45.3 2.2 %collective-permute-done.7 = bf16[1,48,512]{2,1,0:T(8,128)(2,1)S(1)} collective-permute-done((bf16[1,48,512]{2,1,0:T(8,128)(2,1)S(1)}, bf16[1,48,512]{2,1,0:T(8,128)(2,1)S(1)}, u32[]{:S(2)}, u32[]{:S(2)}) %collective-permute-start.7) | collective-permute-done | bytes 49184 | tf_op jit(solution)/shard_map/ppermute | solution.py:19
  47.5 2.6 %collective-permute-start.10 = (bf16[1,48,512]{2,1,0:T(8,128)(2,1)S(1)}, bf16[1,48,512]{2,1,0:T(8,128)(2,1)S(1)}, u32[]{:S(2)}, u32[]{:S(2)}) collective-permute-start(bf16[1,48,512]{2,1,0:T(8,128)(2,1)S(1)} %collective-permute-done.8), channel_id=1, source_target_pairs={{0,28},{4,0},{8,4},{12,8},{16,12},{20,16},{24,20},{28,24},{1,29},{... | collective-permute-start | bytes 147464 | tf_op jit(solution)/shard_map/ppermute | solution.py:24
  52.0 2.8 %collective-permute-start.12 = (bf16[1,48,512]{2,1,0:T(8,128)(2,1)S(1)}, bf16[1,48,512]{2,1,0:T(8,128)(2,1)S(1)}, u32[]{:S(2)}, u32[]{:S(2)}) collective-permute-start(bf16[1,48,512]{2,1,0:T(8,128)(2,1)S(1)} %collective-permute-done.10), channel_id=1, source_target_pairs={{0,28},{4,0},{8,4},{12,8},{16,12},{20,16},{24,20},{28,24},{1,29},{... | collective-permute-start | bytes 147464 | tf_op jit(solution)/shard_map/ppermute | solution.py:24
  57.6 3.2 %collective-permute-done.13 = bf16[1,48,512]{2,1,0:T(8,128)(2,1)S(1)} collective-permute-done((bf16[1,48,512]{2,1,0:T(8,128)(2,1)S(1)}, bf16[1,48,512]{2,1,0:T(8,128)(2,1)S(1)}, u32[]{:S(2)}, u32[]{:S(2)}) %collective-permute-start.13) | collective-permute-done | bytes 49184 | tf_op jit(solution)/shard_map/ppermute | solution.py:19
  63.4 6.6 %while.20 = (s32[]{:T(128)}, f32[48,512]{1,0:T(8,128)S(1)}, s32[]{:T(128)}, f32[512,512]{1,0:T(8,128)S(1)}, f32[8,48,512]{2,1,0:T(8,128)}, /*index=5*/s32[]{:T(128)}, s32[]{:T(128)}, s32[]{:T(128)}) while((s32[]{:T(128)}, f32[48,512]{1,0:T(8,128)S(1)}, s32[]{:T(128)}, f32[512,512]{1,0:T(8,128)S(1)}, f32[8,48,512]{2,1,0:T(8,128)}, ...), condition=%wide.region_1.2_spmd, body=%wide.region_0.1_spmd.sunk | while | flops 151019520 | bytes 1540227 | solution.py:105
  70.9 1.9 %collective-permute-start.14 = (f32[48,512]{1,0:T(8,128)S(1)}, f32[48,512]{1,0:T(8,128)S(1)}, u32[]{:S(2)}, u32[]{:S(2)}) collective-permute-start(f32[48,512]{1,0:T(8,128)S(1)} %add.525), channel_id=1, source_target_pairs={{0,4},{4,8},{8,12},{12,16},{16,20},{20,24},{24,28},{1,5},{5,9},{9,... | collective-permute-start | bytes 294920 | tf_op jit(solution)/shard_map/ppermute | solution.py:50
  72.8 4.9 %collective-permute-done.14 = f32[48,512]{1,0:T(8,128)S(1)} collective-permute-done((f32[48,512]{1,0:T(8,128)S(1)}, f32[48,512]{1,0:T(8,128)S(1)}, u32[]{:S(2)}, u32[]{:S(2)}) %collective-permute-start.14) | collective-permute-done | bytes 98336 | tf_op jit(solution)/shard_map/ppermute | solution.py:50
  77.9 2.0 %collective-permute-start.15 = (f32[8,512]{1,0:T(8,128)S(1)}, f32[8,512]{1,0:T(8,128)S(1)}, u32[]{:S(2)}, u32[]{:S(2)}) collective-permute-start(f32[8,512]{1,0:T(8,128)S(1)} %get-tuple-element.97), channel_id=1, source_target_pairs={{0,1},{1,2},{2,3},{3,0},{4,5},{5,6},{6,7},{7,4},{8,9},{9,10},{10,1... | collective-permute-start | bytes 49160 | tf_op jit(solution)/shard_map/ppermute | solution.py:38
  81.6 1.9 %collective-permute-done.15 = f32[8,512]{1,0:T(8,128)S(1)} collective-permute-done((f32[8,512]{1,0:T(8,128)S(1)}, f32[8,512]{1,0:T(8,128)S(1)}, u32[]{:S(2)}, u32[]{:S(2)}) %collective-permute-start.15) | collective-permute-done | bytes 16416 | tf_op jit(solution)/shard_map/ppermute | solution.py:38
  90.0 1.9 %collective-permute-start.17 = (f32[48,512]{1,0:T(8,128)S(1)}, f32[48,512]{1,0:T(8,128)S(1)}, u32[]{:S(2)}, u32[]{:S(2)}) collective-permute-start(f32[48,512]{1,0:T(8,128)S(1)} %fusion.185), channel_id=1, source_target_pairs={{0,4},{4,8},{8,12},{12,16},{16,20},{20,24},{24,28},{1,5},{5,9},{9,... | collective-permute-start | bytes 294920 | tf_op jit(solution)/shard_map/ppermute | solution.py:50
  91.9 4.9 %collective-permute-done.17 = f32[48,512]{1,0:T(8,128)S(1)} collective-permute-done((f32[48,512]{1,0:T(8,128)S(1)}, f32[48,512]{1,0:T(8,128)S(1)}, u32[]{:S(2)}, u32[]{:S(2)}) %collective-permute-start.17) | collective-permute-done | bytes 98336 | tf_op jit(solution)/shard_map/ppermute | solution.py:50
  96.9 2.0 %collective-permute-start.18 = (f32[8,512]{1,0:T(8,128)S(1)}, f32[8,512]{1,0:T(8,128)S(1)}, u32[]{:S(2)}, u32[]{:S(2)}) collective-permute-start(f32[8,512]{1,0:T(8,128)S(1)} %get-tuple-element.95), channel_id=1, source_target_pairs={{0,1},{1,2},{2,3},{3,0},{4,5},{5,6},{6,7},{7,4},{8,9},{9,10},{10,1... | collective-permute-start | bytes 49160 | tf_op jit(solution)/shard_map/ppermute | solution.py:38
  100.6 2.1 %collective-permute-done.18 = f32[8,512]{1,0:T(8,128)S(1)} collective-permute-done((f32[8,512]{1,0:T(8,128)S(1)}, f32[8,512]{1,0:T(8,128)S(1)}, u32[]{:S(2)}, u32[]{:S(2)}) %collective-permute-start.18) | collective-permute-done | bytes 16416 | tf_op jit(solution)/shard_map/ppermute | solution.py:38
  110.0 2.6 %collective-permute-start.21 = (bf16[1,48,512]{2,1,0:T(8,128)(2,1)S(1)}, bf16[1,48,512]{2,1,0:T(8,128)(2,1)S(1)}, u32[]{:S(2)}, u32[]{:S(2)}) collective-permute-start(bf16[1,48,512]{2,1,0:T(8,128)(2,1)S(1)} %get-tuple-element.108), channel_id=1, source_target_pairs={{0,28},{4,0},{8,4},{12,8},{16,12},{20,16},{24,20},{28,24},{1,29},{... | collective-permute-start | bytes 147464 | tf_op jit(solution)/shard_map/ppermute | solution.py:24
  112.6 1.8 %collective-permute-done.20 = bf16[1,48,512]{2,1,0:T(8,128)(2,1)S(1)} collective-permute-done((bf16[1,48,512]{2,1,0:T(8,128)(2,1)S(1)}, bf16[1,48,512]{2,1,0:T(8,128)(2,1)S(1)}, u32[]{:S(2)}, u32[]{:S(2)}) %collective-permute-start.20) | collective-permute-done | bytes 49184 | tf_op jit(solution)/shard_map/ppermute | solution.py:19
  115.0 2.6 %collective-permute-start.23 = (bf16[1,48,512]{2,1,0:T(8,128)(2,1)S(1)}, bf16[1,48,512]{2,1,0:T(8,128)(2,1)S(1)}, u32[]{:S(2)}, u32[]{:S(2)}) collective-permute-start(bf16[1,48,512]{2,1,0:T(8,128)(2,1)S(1)} %collective-permute-done.21), channel_id=1, source_target_pairs={{0,28},{4,0},{8,4},{12,8},{16,12},{20,16},{24,20},{28,24},{1,29},{... | collective-permute-start | bytes 147464 | tf_op jit(solution)/shard_map/ppermute | solution.py:24
  119.5 2.6 %collective-permute-start.25 = (bf16[1,48,512]{2,1,0:T(8,128)(2,1)S(1)}, bf16[1,48,512]{2,1,0:T(8,128)(2,1)S(1)}, u32[]{:S(2)}, u32[]{:S(2)}) collective-permute-start(bf16[1,48,512]{2,1,0:T(8,128)(2,1)S(1)} %collective-permute-done.23), channel_id=1, source_target_pairs={{0,28},{4,0},{8,4},{12,8},{16,12},{20,16},{24,20},{28,24},{1,29},{... | collective-permute-start | bytes 147464 | tf_op jit(solution)/shard_map/ppermute | solution.py:24
  124.5 3.2 %collective-permute-done.26 = bf16[1,48,512]{2,1,0:T(8,128)(2,1)S(1)} collective-permute-done((bf16[1,48,512]{2,1,0:T(8,128)(2,1)S(1)}, bf16[1,48,512]{2,1,0:T(8,128)(2,1)S(1)}, u32[]{:S(2)}, u32[]{:S(2)}) %collective-permute-start.26) | collective-permute-done | bytes 49184 | tf_op jit(solution)/shard_map/ppermute | solution.py:19
  130.3 6.6 %while.21 = (s32[]{:T(128)}, f32[48,512]{1,0:T(8,128)S(1)}, s32[]{:T(128)}, f32[512,512]{1,0:T(8,128)S(1)}, f32[8,48,512]{2,1,0:T(8,128)}, /*index=5*/s32[]{:T(128)}, s32[]{:T(128)}, s32[]{:T(128)}) while((s32[]{:T(128)}, f32[48,512]{1,0:T(8,128)S(1)}, s32[]{:T(128)}, f32[512,512]{1,0:T(8,128)S(1)}, f32[8,48,512]{2,1,0:T(8,128)}, ...), condition=%wide.region_3.4_spmd, body=%wide.region_2.3_spmd.sunk | while | flops 151019520 | bytes 1540227 | solution.py:105
  136.9 1.9 %collective-permute-start.27 = (f32[48,512]{1,0:T(8,128)S(1)}, f32[48,512]{1,0:T(8,128)S(1)}, u32[]{:S(2)}, u32[]{:S(2)}) collective-permute-start(f32[48,512]{1,0:T(8,128)S(1)} %add.574), channel_id=1, source_target_pairs={{0,4},{4,8},{8,12},{12,16},{16,20},{20,24},{24,28},{1,5},{5,9},{9,... | collective-permute-start | bytes 294920 | tf_op jit(solution)/shard_map/ppermute | solution.py:50
  138.9 4.9 %collective-permute-done.27 = f32[48,512]{1,0:T(8,128)S(1)} collective-permute-done((f32[48,512]{1,0:T(8,128)S(1)}, f32[48,512]{1,0:T(8,128)S(1)}, u32[]{:S(2)}, u32[]{:S(2)}) %collective-permute-start.27) | collective-permute-done | bytes 98336 | tf_op jit(solution)/shard_map/ppermute | solution.py:50
  143.9 2.0 %collective-permute-start.28 = (f32[8,512]{1,0:T(8,128)S(1)}, f32[8,512]{1,0:T(8,128)S(1)}, u32[]{:S(2)}, u32[]{:S(2)}) collective-permute-start(f32[8,512]{1,0:T(8,128)S(1)} %get-tuple-element.93), channel_id=1, source_target_pairs={{0,1},{1,2},{2,3},{3,0},{4,5},{5,6},{6,7},{7,4},{8,9},{9,10},{10,1... | collective-permute-start | bytes 49160 | tf_op jit(solution)/shard_map/ppermute | solution.py:38
  147.6 1.9 %collective-permute-done.28 = f32[8,512]{1,0:T(8,128)S(1)} collective-permute-done((f32[8,512]{1,0:T(8,128)S(1)}, f32[8,512]{1,0:T(8,128)S(1)}, u32[]{:S(2)}, u32[]{:S(2)}) %collective-permute-start.28) | collective-permute-done | bytes 16416 | tf_op jit(solution)/shard_map/ppermute | solution.py:38
  (170 shorter events, 74.1 us)
Async XLA Ops:
  0.1 8.5 %collective-permute-start.3 = (f32[8,512]{1,0:T(8,128)S(1)}, f32[8,512]{1,0:T(8,128)S(1)}, u32[]{:S(2)}, u32[]{:S(2)}) collective-permute-start(f32[8,512]{1,0:T(8,128)S(1)} %get-tuple-element.102), channel_id=1, source_target_pairs={{1,0},{2,1},{3,2},{0,3},{5,4},{6,5},{7,6},{4,7},{9,8},{10,9},{11,1... | collective-permute-start | bytes 49160 | tf_op jit(solution)/shard_map/ppermute | solution.py:40
  3.7 5.7 %collective-permute-start.2 = (f32[8,512]{1,0:T(8,128)S(1)}, f32[8,512]{1,0:T(8,128)S(1)}, u32[]{:S(2)}, u32[]{:S(2)}) collective-permute-start(f32[8,512]{1,0:T(8,128)S(1)} %get-tuple-element.101), channel_id=1, source_target_pairs={{0,1},{1,2},{2,3},{3,0},{4,5},{5,6},{6,7},{7,4},{8,9},{9,10},{10,1... | collective-permute-start | bytes 49160 | tf_op jit(solution)/shard_map/ppermute | solution.py:38
  4.7 5.9 %collective-permute-start.1 = (bf16[10,8,512]{2,1,0:T(8,128)(2,1)S(1)}, bf16[10,8,512]{2,1,0:T(8,128)(2,1)S(1)}, u32[]{:S(2)}, u32[]{:S(2)}) collective-permute-start(bf16[10,8,512]{2,1,0:T(8,128)(2,1)S(1)} %get-tuple-element.89), channel_id=1, source_target_pairs={{1,0},{2,1},{3,2},{0,3},{5,4},{6,5},{7,6},{4,7},{9,8},{10,9},{11,1... | collective-permute-start | bytes 245768 | tf_op jit(solution)/shard_map/ppermute | solution.py:40
  8.5 6.2 %collective-permute-start = (bf16[10,8,512]{2,1,0:T(8,128)(2,1)S(1)}, bf16[10,8,512]{2,1,0:T(8,128)(2,1)S(1)}, u32[]{:S(2)}, u32[]{:S(2)}) collective-permute-start(bf16[10,8,512]{2,1,0:T(8,128)(2,1)S(1)} %get-tuple-element.88), channel_id=1, source_target_pairs={{0,1},{1,2},{2,3},{3,0},{4,5},{5,6},{6,7},{7,4},{8,9},{9,10},{10,1... | collective-permute-start | bytes 245768 | tf_op jit(solution)/shard_map/ppermute | solution.py:38
  20.6 19.0 %copy-start.9 = (bf16[50,512]{1,0:T(8,128)(2,1)}, bf16[50,512]{1,0:T(8,128)(2,1)S(1)}, u32[]{:S(2)}) copy-start(bf16[50,512]{1,0:T(8,128)(2,1)S(1)} %get-tuple-element.84) | copy-start | bytes 153604
  22.2 19.1 %copy-start.11 = (f32[48,512]{1,0:T(8,128)}, f32[48,512]{1,0:T(8,128)S(1)}, u32[]{:S(2)}) copy-start(f32[48,512]{1,0:T(8,128)S(1)} %fusion.184) | copy-start | bytes 294916
  22.2 6.8 %collective-permute-start.4 = (f32[48,512]{1,0:T(8,128)S(1)}, f32[48,512]{1,0:T(8,128)S(1)}, u32[]{:S(2)}, u32[]{:S(2)}) collective-permute-start(f32[48,512]{1,0:T(8,128)S(1)} %fusion.184), channel_id=1, source_target_pairs={{0,4},{4,8},{8,12},{12,16},{16,20},{20,24},{24,28},{1,5},{5,9},{9,... | collective-permute-start | bytes 294920 | tf_op jit(solution)/shard_map/ppermute | solution.py:50
  29.1 3.8 %collective-permute-start.6 = (f32[8,512]{1,0:T(8,128)S(1)}, f32[8,512]{1,0:T(8,128)S(1)}, u32[]{:S(2)}, u32[]{:S(2)}) collective-permute-start(f32[8,512]{1,0:T(8,128)S(1)} %get-tuple-element.100), channel_id=1, source_target_pairs={{1,0},{2,1},{3,2},{0,3},{5,4},{6,5},{7,6},{4,7},{9,8},{10,9},{11,1... | collective-permute-start | bytes 49160 | tf_op jit(solution)/shard_map/ppermute | solution.py:40
  29.2 5.5 %collective-permute-start.5 = (f32[8,512]{1,0:T(8,128)S(1)}, f32[8,512]{1,0:T(8,128)S(1)}, u32[]{:S(2)}, u32[]{:S(2)}) collective-permute-start(f32[8,512]{1,0:T(8,128)S(1)} %get-tuple-element.99), channel_id=1, source_target_pairs={{0,1},{1,2},{2,3},{3,0},{4,5},{5,6},{6,7},{7,4},{8,9},{9,10},{10,1... | collective-permute-start | bytes 49160 | tf_op jit(solution)/shard_map/ppermute | solution.py:38
  42.6 4.9 %collective-permute-start.7 = (bf16[1,48,512]{2,1,0:T(8,128)(2,1)S(1)}, bf16[1,48,512]{2,1,0:T(8,128)(2,1)S(1)}, u32[]{:S(2)}, u32[]{:S(2)}) collective-permute-start(bf16[1,48,512]{2,1,0:T(8,128)(2,1)S(1)} %get-tuple-element.106), channel_id=1, source_target_pairs={{0,4},{4,8},{8,12},{12,16},{16,20},{20,24},{24,28},{28,0},{1,5},{5... | collective-permute-start | bytes 147464 | tf_op jit(solution)/shard_map/ppermute | solution.py:19
  42.6 4.9 %collective-permute-start.8 = (bf16[1,48,512]{2,1,0:T(8,128)(2,1)S(1)}, bf16[1,48,512]{2,1,0:T(8,128)(2,1)S(1)}, u32[]{:S(2)}, u32[]{:S(2)}) collective-permute-start(bf16[1,48,512]{2,1,0:T(8,128)(2,1)S(1)} %get-tuple-element.106), channel_id=1, source_target_pairs={{0,28},{4,0},{8,4},{12,8},{16,12},{20,16},{24,20},{28,24},{1,29},{... | collective-permute-start | bytes 147464 | tf_op jit(solution)/shard_map/ppermute | solution.py:24
  47.5 4.4 %collective-permute-start.9 = (bf16[1,48,512]{2,1,0:T(8,128)(2,1)S(1)}, bf16[1,48,512]{2,1,0:T(8,128)(2,1)S(1)}, u32[]{:S(2)}, u32[]{:S(2)}) collective-permute-start(bf16[1,48,512]{2,1,0:T(8,128)(2,1)S(1)} %collective-permute-done.7), channel_id=1, source_target_pairs={{0,4},{4,8},{8,12},{12,16},{16,20},{20,24},{24,28},{28,0},{1,5},{5... | collective-permute-start | bytes 147464 | tf_op jit(solution)/shard_map/ppermute | solution.py:19
  47.5 4.4 %collective-permute-start.10 = (bf16[1,48,512]{2,1,0:T(8,128)(2,1)S(1)}, bf16[1,48,512]{2,1,0:T(8,128)(2,1)S(1)}, u32[]{:S(2)}, u32[]{:S(2)}) collective-permute-start(bf16[1,48,512]{2,1,0:T(8,128)(2,1)S(1)} %collective-permute-done.8), channel_id=1, source_target_pairs={{0,28},{4,0},{8,4},{12,8},{16,12},{20,16},{24,20},{28,24},{1,29},{... | collective-permute-start | bytes 147464 | tf_op jit(solution)/shard_map/ppermute | solution.py:24
  51.9 4.4 %collective-permute-start.11 = (bf16[1,48,512]{2,1,0:T(8,128)(2,1)S(1)}, bf16[1,48,512]{2,1,0:T(8,128)(2,1)S(1)}, u32[]{:S(2)}, u32[]{:S(2)}) collective-permute-start(bf16[1,48,512]{2,1,0:T(8,128)(2,1)S(1)} %collective-permute-done.9), channel_id=1, source_target_pairs={{0,4},{4,8},{8,12},{12,16},{16,20},{20,24},{24,28},{28,0},{1,5},{5... | collective-permute-start | bytes 147464 | tf_op jit(solution)/shard_map/ppermute | solution.py:19
  52.0 5.0 %collective-permute-start.12 = (bf16[1,48,512]{2,1,0:T(8,128)(2,1)S(1)}, bf16[1,48,512]{2,1,0:T(8,128)(2,1)S(1)}, u32[]{:S(2)}, u32[]{:S(2)}) collective-permute-start(bf16[1,48,512]{2,1,0:T(8,128)(2,1)S(1)} %collective-permute-done.10), channel_id=1, source_target_pairs={{0,28},{4,0},{8,4},{12,8},{16,12},{20,16},{24,20},{28,24},{1,29},{... | collective-permute-start | bytes 147464 | tf_op jit(solution)/shard_map/ppermute | solution.py:24
  56.3 4.4 %collective-permute-start.13 = (bf16[1,48,512]{2,1,0:T(8,128)(2,1)S(1)}, bf16[1,48,512]{2,1,0:T(8,128)(2,1)S(1)}, u32[]{:S(2)}, u32[]{:S(2)}) collective-permute-start(bf16[1,48,512]{2,1,0:T(8,128)(2,1)S(1)} %collective-permute-done.11), channel_id=1, source_target_pairs={{0,4},{4,8},{8,12},{12,16},{16,20},{20,24},{24,28},{28,0},{1,5},{5... | collective-permute-start | bytes 147464 | tf_op jit(solution)/shard_map/ppermute | solution.py:19
  70.9 6.8 %collective-permute-start.14 = (f32[48,512]{1,0:T(8,128)S(1)}, f32[48,512]{1,0:T(8,128)S(1)}, u32[]{:S(2)}, u32[]{:S(2)}) collective-permute-start(f32[48,512]{1,0:T(8,128)S(1)} %add.525), channel_id=1, source_target_pairs={{0,4},{4,8},{8,12},{12,16},{16,20},{20,24},{24,28},{1,5},{5,9},{9,... | collective-permute-start | bytes 294920 | tf_op jit(solution)/shard_map/ppermute | solution.py:50
  77.8 3.8 %collective-permute-start.16 = (f32[8,512]{1,0:T(8,128)S(1)}, f32[8,512]{1,0:T(8,128)S(1)}, u32[]{:S(2)}, u32[]{:S(2)}) collective-permute-start(f32[8,512]{1,0:T(8,128)S(1)} %get-tuple-element.98), channel_id=1, source_target_pairs={{1,0},{2,1},{3,2},{0,3},{5,4},{6,5},{7,6},{4,7},{9,8},{10,9},{11,1... | collective-permute-start | bytes 49160 | tf_op jit(solution)/shard_map/ppermute | solution.py:40
  77.9 5.6 %collective-permute-start.15 = (f32[8,512]{1,0:T(8,128)S(1)}, f32[8,512]{1,0:T(8,128)S(1)}, u32[]{:S(2)}, u32[]{:S(2)}) collective-permute-start(f32[8,512]{1,0:T(8,128)S(1)} %get-tuple-element.97), channel_id=1, source_target_pairs={{0,1},{1,2},{2,3},{3,0},{4,5},{5,6},{6,7},{7,4},{8,9},{9,10},{10,1... | collective-permute-start | bytes 49160 | tf_op jit(solution)/shard_map/ppermute | solution.py:38
  90.0 6.8 %collective-permute-start.17 = (f32[48,512]{1,0:T(8,128)S(1)}, f32[48,512]{1,0:T(8,128)S(1)}, u32[]{:S(2)}, u32[]{:S(2)}) collective-permute-start(f32[48,512]{1,0:T(8,128)S(1)} %fusion.185), channel_id=1, source_target_pairs={{0,4},{4,8},{8,12},{12,16},{16,20},{20,24},{24,28},{1,5},{5,9},{9,... | collective-permute-start | bytes 294920 | tf_op jit(solution)/shard_map/ppermute | solution.py:50
  96.8 3.8 %collective-permute-start.19 = (f32[8,512]{1,0:T(8,128)S(1)}, f32[8,512]{1,0:T(8,128)S(1)}, u32[]{:S(2)}, u32[]{:S(2)}) collective-permute-start(f32[8,512]{1,0:T(8,128)S(1)} %get-tuple-element.96), channel_id=1, source_target_pairs={{1,0},{2,1},{3,2},{0,3},{5,4},{6,5},{7,6},{4,7},{9,8},{10,9},{11,1... | collective-permute-start | bytes 49160 | tf_op jit(solution)/shard_map/ppermute | solution.py:40
  96.9 5.8 %collective-permute-start.18 = (f32[8,512]{1,0:T(8,128)S(1)}, f32[8,512]{1,0:T(8,128)S(1)}, u32[]{:S(2)}, u32[]{:S(2)}) collective-permute-start(f32[8,512]{1,0:T(8,128)S(1)} %get-tuple-element.95), channel_id=1, source_target_pairs={{0,1},{1,2},{2,3},{3,0},{4,5},{5,6},{6,7},{7,4},{8,9},{9,10},{10,1... | collective-permute-start | bytes 49160 | tf_op jit(solution)/shard_map/ppermute | solution.py:38
  110.0 4.4 %collective-permute-start.20 = (bf16[1,48,512]{2,1,0:T(8,128)(2,1)S(1)}, bf16[1,48,512]{2,1,0:T(8,128)(2,1)S(1)}, u32[]{:S(2)}, u32[]{:S(2)}) collective-permute-start(bf16[1,48,512]{2,1,0:T(8,128)(2,1)S(1)} %get-tuple-element.108), channel_id=1, source_target_pairs={{0,4},{4,8},{8,12},{12,16},{16,20},{20,24},{24,28},{28,0},{1,5},{5... | collective-permute-start | bytes 147464 | tf_op jit(solution)/shard_map/ppermute | solution.py:19
  110.0 5.0 %collective-permute-start.21 = (bf16[1,48,512]{2,1,0:T(8,128)(2,1)S(1)}, bf16[1,48,512]{2,1,0:T(8,128)(2,1)S(1)}, u32[]{:S(2)}, u32[]{:S(2)}) collective-permute-start(bf16[1,48,512]{2,1,0:T(8,128)(2,1)S(1)} %get-tuple-element.108), channel_id=1, source_target_pairs={{0,28},{4,0},{8,4},{12,8},{16,12},{20,16},{24,20},{28,24},{1,29},{... | collective-permute-start | bytes 147464 | tf_op jit(solution)/shard_map/ppermute | solution.py:24
  114.4 4.4 %collective-permute-start.22 = (bf16[1,48,512]{2,1,0:T(8,128)(2,1)S(1)}, bf16[1,48,512]{2,1,0:T(8,128)(2,1)S(1)}, u32[]{:S(2)}, u32[]{:S(2)}) collective-permute-start(bf16[1,48,512]{2,1,0:T(8,128)(2,1)S(1)} %collective-permute-done.20), channel_id=1, source_target_pairs={{0,4},{4,8},{8,12},{12,16},{16,20},{20,24},{24,28},{28,0},{1,5},{5... | collective-permute-start | bytes 147464 | tf_op jit(solution)/shard_map/ppermute | solution.py:19
  115.0 4.4 %collective-permute-start.23 = (bf16[1,48,512]{2,1,0:T(8,128)(2,1)S(1)}, bf16[1,48,512]{2,1,0:T(8,128)(2,1)S(1)}, u32[]{:S(2)}, u32[]{:S(2)}) collective-permute-start(bf16[1,48,512]{2,1,0:T(8,128)(2,1)S(1)} %collective-permute-done.21), channel_id=1, source_target_pairs={{0,28},{4,0},{8,4},{12,8},{16,12},{20,16},{24,20},{28,24},{1,29},{... | collective-permute-start | bytes 147464 | tf_op jit(solution)/shard_map/ppermute | solution.py:24
  118.8 4.4 %collective-permute-start.24 = (bf16[1,48,512]{2,1,0:T(8,128)(2,1)S(1)}, bf16[1,48,512]{2,1,0:T(8,128)(2,1)S(1)}, u32[]{:S(2)}, u32[]{:S(2)}) collective-permute-start(bf16[1,48,512]{2,1,0:T(8,128)(2,1)S(1)} %collective-permute-done.22), channel_id=1, source_target_pairs={{0,4},{4,8},{8,12},{12,16},{16,20},{20,24},{24,28},{28,0},{1,5},{5... | collective-permute-start | bytes 147464 | tf_op jit(solution)/shard_map/ppermute | solution.py:19
  119.5 4.4 %collective-permute-start.25 = (bf16[1,48,512]{2,1,0:T(8,128)(2,1)S(1)}, bf16[1,48,512]{2,1,0:T(8,128)(2,1)S(1)}, u32[]{:S(2)}, u32[]{:S(2)}) collective-permute-start(bf16[1,48,512]{2,1,0:T(8,128)(2,1)S(1)} %collective-permute-done.23), channel_id=1, source_target_pairs={{0,28},{4,0},{8,4},{12,8},{16,12},{20,16},{24,20},{28,24},{1,29},{... | collective-permute-start | bytes 147464 | tf_op jit(solution)/shard_map/ppermute | solution.py:24
  123.2 4.4 %collective-permute-start.26 = (bf16[1,48,512]{2,1,0:T(8,128)(2,1)S(1)}, bf16[1,48,512]{2,1,0:T(8,128)(2,1)S(1)}, u32[]{:S(2)}, u32[]{:S(2)}) collective-permute-start(bf16[1,48,512]{2,1,0:T(8,128)(2,1)S(1)} %collective-permute-done.24), channel_id=1, source_target_pairs={{0,4},{4,8},{8,12},{12,16},{16,20},{20,24},{24,28},{28,0},{1,5},{5... | collective-permute-start | bytes 147464 | tf_op jit(solution)/shard_map/ppermute | solution.py:19
  136.9 6.8 %collective-permute-start.27 = (f32[48,512]{1,0:T(8,128)S(1)}, f32[48,512]{1,0:T(8,128)S(1)}, u32[]{:S(2)}, u32[]{:S(2)}) collective-permute-start(f32[48,512]{1,0:T(8,128)S(1)} %add.574), channel_id=1, source_target_pairs={{0,4},{4,8},{8,12},{12,16},{16,20},{20,24},{24,28},{1,5},{5,9},{9,... | collective-permute-start | bytes 294920 | tf_op jit(solution)/shard_map/ppermute | solution.py:50
  143.8 3.8 %collective-permute-start.29 = (f32[8,512]{1,0:T(8,128)S(1)}, f32[8,512]{1,0:T(8,128)S(1)}, u32[]{:S(2)}, u32[]{:S(2)}) collective-permute-start(f32[8,512]{1,0:T(8,128)S(1)} %get-tuple-element.94), channel_id=1, source_target_pairs={{1,0},{2,1},{3,2},{0,3},{5,4},{6,5},{7,6},{4,7},{9,8},{10,9},{11,1... | collective-permute-start | bytes 49160 | tf_op jit(solution)/shard_map/ppermute | solution.py:40
  143.9 5.6 %collective-permute-start.28 = (f32[8,512]{1,0:T(8,128)S(1)}, f32[8,512]{1,0:T(8,128)S(1)}, u32[]{:S(2)}, u32[]{:S(2)}) collective-permute-start(f32[8,512]{1,0:T(8,128)S(1)} %get-tuple-element.93), channel_id=1, source_target_pairs={{0,1},{1,2},{2,3},{3,0},{4,5},{5,6},{6,7},{7,4},{8,9},{9,10},{10,1... | collective-permute-start | bytes 49160 | tf_op jit(solution)/shard_map/ppermute | solution.py:38
  (12 other events, 64.1 us)
